TPU v7x, 256 devices: a whole 4x4x8 slice. The times are simulated.
256 devices in a mesh: dp: 16 (over y, z_hi, core), mp: 16 (over x, z_lo).
Axes of the slice: x: 4, y: 4, z: 8 (z_hi: 2, z_lo: 4; z = z_hi * 4 + z_lo), core: 2. Of those that a mesh axis runs over, the one named last changes fastest.
Arguments:
- skip_stream_arriving: float32 [4096, 2304], P('dp', 'mp'), may hold values from -170 to 170
- chosen_specialists: int32 [4096, 2], P('dp'), may hold values from 0 to 3, all different within a row; in each aligned block of 256 rows (0 to 255, 256 to 511, ...) at most 160 rows name the same one
- sequence_piece_tallies: int32 [16, 4], P('dp'), may hold values from 1 to 128, 256 in all within a row
- premix_rmsnorm_gain: float32 [2304], P('mp'), may hold values from 0.1 to 1.9
- dispatcher_weights: bfloat16 [2304, 4], replicated, may hold values from -0.125 to 0.125
- specialist_switch_weights: bfloat16 [4, 2304, 5760], P(None, 'dp', 'mp'), may hold values from -0.125 to 0.125
- specialist_expand_weights: bfloat16 [4, 2304, 5760], P(None, 'dp', 'mp'), may hold values from -0.125 to 0.125
- specialist_contract_weights: bfloat16 [4, 5760, 2304], P(None, 'mp', 'dp'), may hold values from -0.109375 to 0.109375
- terminal_rmsnorm_gain: float32 [2304], replicated, may hold values from 0.1 to 1.9
- lexicon_projector_weights: bfloat16 [2304, 131072], P(None, ('dp', 'mp')), may hold values from -12 to 12
- softness_per_sequence: float32 [64], replicated, may hold values from 0.02 to 1.5
Outputs:
- new_hidden: float32 [4096, 2304], P('dp', 'mp')
- logprobs: float32 [64, 131072], P(None, ('dp', 'mp'))
Inputs may be any that keep to these rules, and one draw needn't show every extreme that they name: `chosen_specialists`: in the 256 rows of each data group no expert is named by more than 160 rows, a bound that some block reaches. `sequence_piece_tallies`: each row sums to 256; its largest entry is 128.
All inputs are finite; a program needn't handle non-finite values.
Results may differ from a plain program's by a relative error of at most 0.0014.
Values may be sent and summed in bfloat16 or wider, within the bound.
A program may use at most 128 MiB of HBM per device.

v0:
```python
import math
import jax
import jax.numpy as jnp
from jax import lax
from jax.sharding import PartitionSpec as P

EMBED_DIMENSION = 2304
CAP = 160
branch_scale = 1.4 / math.sqrt(40.0)
epsilon = 1e-05


def slot_tables(routes_grp, expert, capacity):
    count = routes_grp.shape[0]
    hit = jnp.any(routes_grp == expert, axis=1)
    second = (routes_grp[:, 1] == expert).astype(jnp.int32)
    order = jnp.cumsum(hit.astype(jnp.int32), dtype=jnp.int32) - 1
    target = jnp.where(hit, order, capacity)
    tokens = jnp.arange(count, dtype=jnp.int32)
    slot_rows = jnp.zeros((capacity,), jnp.int32).at[target].set(tokens, mode="drop")
    live = jnp.zeros((capacity,), jnp.float32).at[target].set(1.0, mode="drop")
    which = jnp.zeros((capacity,), jnp.int32).at[target].set(second, mode="drop")
    return (slot_rows, live, which)


def body(
    skip_stream_arriving,
    chosen_specialists,
    sequence_piece_tallies,
    premix_rmsnorm_gain,
    dispatcher_weights,
    specialist_switch_weights,
    specialist_expand_weights,
    specialist_contract_weights,
    terminal_rmsnorm_gain,
    lexicon_projector_weights,
    softness_per_sequence,
):
    tok_rows = skip_stream_arriving.shape[0]
    local_width = skip_stream_arriving.shape[1]
    experts = specialist_switch_weights.shape[0]
    unit_cols = specialist_switch_weights.shape[2]
    squares = lax.psum(jnp.sum(skip_stream_arriving * skip_stream_arriving, axis=1), "mp")
    normed_local = (
        skip_stream_arriving
        * lax.rsqrt(squares / EMBED_DIMENSION + epsilon)[:, None]
        * premix_rmsnorm_gain
    ).astype(jnp.bfloat16)
    features = lax.all_gather(normed_local, "mp", axis=1, tiled=True)
    router = jnp.dot(features, dispatcher_weights, preferred_element_type=jnp.float32)
    mixing = jax.nn.softmax(jnp.take_along_axis(router, chosen_specialists, axis=1), axis=1)
    tables = [slot_tables(chosen_specialists, expert, CAP) for expert in range(experts)]
    inputs = jnp.stack([features[table[0]] for table in tables])
    scales = jnp.stack([mixing[table[0], table[2]] * table[1] for table in tables])
    pieces_out = []
    for expert in range(experts):
        rows_in = inputs[expert]

        def add_pair(carry, pieces, start, rows_in=rows_in):
            return (
                jnp.dot(rows_in, pieces[0], preferred_element_type=jnp.float32),
                jnp.dot(rows_in, pieces[1], preferred_element_type=jnp.float32),
            )

        empty = jnp.zeros((CAP, unit_cols), jnp.float32)
        gate, up_part = add_pair(
            (empty, empty),
            (
                lax.all_gather(specialist_switch_weights[expert], "dp", axis=0, tiled=True),
                lax.all_gather(specialist_expand_weights[expert], "dp", axis=0, tiled=True),
            ),
            jnp.int32(0),
        )
        act = (jax.nn.silu(gate) * up_part).astype(jnp.bfloat16)

        def project(piece, start, act=act):
            return jnp.dot(act, piece, preferred_element_type=jnp.float32)

        pieces_out.append(
            project(
                lax.all_gather(specialist_contract_weights[expert], "dp", axis=1, tiled=True),
                jnp.int32(0),
            )
        )
    outputs = jnp.stack(pieces_out)
    combined = jnp.zeros((tok_rows, EMBED_DIMENSION), jnp.float32)
    for expert in range(experts):
        combined = combined.at[tables[expert][0]].add(outputs[expert] * scales[expert][:, None])
    branch = lax.psum_scatter(
        combined.astype(jnp.bfloat16), "mp", scatter_dimension=1, tiled=True
    ).astype(jnp.float32)
    new_hidden = skip_stream_arriving + branch_scale * branch
    ends_index = jnp.cumsum(sequence_piece_tallies[0], dtype=jnp.int32) - 1
    end_local = new_hidden[ends_index]
    groups = lax.axis_size("dp")
    columns_count = lax.axis_size("mp")
    req_count = ends_index.shape[0]
    end_squares = lax.psum(jnp.sum(end_local * end_local, axis=1), "mp")
    gain_local = lax.dynamic_slice_in_dim(
        terminal_rmsnorm_gain, lax.axis_index("mp") * local_width, local_width
    )
    end_normed = (
        end_local * lax.rsqrt(end_squares / EMBED_DIMENSION + epsilon)[:, None] * gain_local
    ).astype(jnp.bfloat16)
    shaped = lax.all_gather(end_normed[None], ("dp", "mp"), axis=0, tiled=True).reshape(
        groups, columns_count, req_count, local_width
    )
    lexicon_projector_feed = shaped.transpose(0, 2, 1, 3).reshape(
        groups * req_count, columns_count * local_width
    )
    lexicon_logit_values = jnp.dot(
        lexicon_projector_feed, lexicon_projector_weights, preferred_element_type=jnp.float32
    ) / (EMBED_DIMENSION / 256.0 * softness_per_sequence[:, None])
    largest = lax.pmax(jnp.max(lexicon_logit_values, axis=1), ("dp", "mp"))
    total_exp = lax.psum(
        jnp.sum(jnp.exp(lexicon_logit_values - largest[:, None]), axis=1), ("dp", "mp")
    )
    logprobs = lexicon_logit_values - largest[:, None] - jnp.log(total_exp)[:, None]
    return (new_hidden, logprobs)


def solution(mesh):
    return jax.shard_map(
        body,
        mesh=mesh,
        in_specs=(
            P("dp", "mp"),
            P("dp", None),
            P("dp", None),
            P("mp"),
            P(),
            P(None, "dp", "mp"),
            P(None, "dp", "mp"),
            P(None, "mp", "dp"),
            P(),
            P(None, ("dp", "mp")),
            P(),
        ),
        out_specs=(P("dp", "mp"), P(None, ("dp", "mp"))),
        check_vma=False,
    )
```

profile of v0, /device:TPU:1, one launch (start us, length us, event | category | flops | bytes accessed | tf_op | source)
XLA Modules:
  0.0 1764.0 jit_solution(12189918322459456357)
XLA Ops:
  8.4 38.4 %psum.21 = f32[256]{0:T(256)S(1)} all-reduce(f32[256]{0:T(256)S(1)} %multiply_reduce_fusion), channel_id=1, replica_groups=mesh['dp'=16,'mp'=16] {'mp'}, use_global_device_ids=true, to_apply=%region_5.6 | all-reduce | flops 256 | bytes 2048 | tf_op jit(solution)/shard_map/psum | solution.py:43
  84.2 43.0 %all-gather.26.cloned.1.call-done = bf16[256,2304]{0,1:T(8,128)(2,1)} async-done(((bf16[256,144]{0,1:T(8,128)(2,1)}), bf16[256,2304]{0,1:T(8,128)(2,1)}) %all-gather.26.cloned.1.call-update) | async-done | bytes 1179664 | tf_op jit(solution)/shard_map/all_gather | solution.py:49
  128.7 4.9 gather_fusion.9
  157.0 42.0 %all-gather.28.cloned.1.call-done = bf16[1,2304,360]{2,1,0:T(8,128)(2,1)} async-done(((bf16[1,144,360]{2,1,0:T(8,128)(2,1)}), bf16[1,2304,360]{2,1,0:T(8,128)(2,1)}) %all-gather.28.cloned.1.call-update) | async-done | bytes 1658896 | tf_op jit(solution)/shard_map/all_gather | solution.py:69
  201.2 56.7 %all-gather.30.cloned.1.call-done = bf16[1,2304,360]{2,1,0:T(8,128)(2,1)} async-done(((bf16[1,144,360]{2,1,0:T(8,128)(2,1)}), bf16[1,2304,360]{2,1,0:T(8,128)(2,1)}) %all-gather.30.cloned.1.call-update) | async-done | bytes 1658896 | tf_op jit(solution)/shard_map/all_gather | solution.py:70
  257.9 58.8 %all-gather.32.cloned.1.call-done = bf16[1,360,2304]{1,2,0:T(8,128)(2,1)} async-done(((bf16[1,360,144]{1,2,0:T(8,128)(2,1)}), bf16[1,360,2304]{1,2,0:T(8,128)(2,1)}) %all-gather.32.cloned.1.call-update) | async-done | bytes 1658896 | tf_op jit(solution)/shard_map/all_gather | solution.py:81
  321.2 5.2 scatter_custom_fusion.3
  326.4 49.2 %all-gather.34.cloned.1.call-done = bf16[1,2304,360]{2,1,0:T(8,128)(2,1)} async-done(((bf16[1,144,360]{2,1,0:T(8,128)(2,1)}), bf16[1,2304,360]{2,1,0:T(8,128)(2,1)}) %all-gather.34.cloned.1.call-update) | async-done | bytes 1658896 | tf_op jit(solution)/shard_map/all_gather | solution.py:69
  377.6 56.8 %all-gather.36.cloned.1.call-done = bf16[1,2304,360]{2,1,0:T(8,128)(2,1)} async-done(((bf16[1,144,360]{2,1,0:T(8,128)(2,1)}), bf16[1,2304,360]{2,1,0:T(8,128)(2,1)}) %all-gather.36.cloned.1.call-update) | async-done | bytes 1658896 | tf_op jit(solution)/shard_map/all_gather | solution.py:70
  434.4 59.5 %all-gather.38.cloned.1.call-done = bf16[1,360,2304]{1,2,0:T(8,128)(2,1)} async-done(((bf16[1,360,144]{1,2,0:T(8,128)(2,1)}), bf16[1,360,2304]{1,2,0:T(8,128)(2,1)}) %all-gather.38.cloned.1.call-update) | async-done | bytes 1658896 | tf_op jit(solution)/shard_map/all_gather | solution.py:81
  498.4 6.6 scatter_fusion
  504.9 48.0 %all-gather.40.cloned.1.call-done = bf16[1,2304,360]{2,1,0:T(8,128)(2,1)} async-done(((bf16[1,144,360]{2,1,0:T(8,128)(2,1)}), bf16[1,2304,360]{2,1,0:T(8,128)(2,1)}) %all-gather.40.cloned.1.call-update) | async-done | bytes 1658896 | tf_op jit(solution)/shard_map/all_gather | solution.py:69
  555.0 56.9 %all-gather.42.cloned.1.call-done = bf16[1,2304,360]{2,1,0:T(8,128)(2,1)} async-done(((bf16[1,144,360]{2,1,0:T(8,128)(2,1)}), bf16[1,2304,360]{2,1,0:T(8,128)(2,1)}) %all-gather.42.cloned.1.call-update) | async-done | bytes 1658896 | tf_op jit(solution)/shard_map/all_gather | solution.py:70
  611.9 58.8 %all-gather.44.cloned.1.call-done = bf16[1,360,2304]{1,2,0:T(8,128)(2,1)} async-done(((bf16[1,360,144]{1,2,0:T(8,128)(2,1)}), bf16[1,360,2304]{1,2,0:T(8,128)(2,1)}) %all-gather.44.cloned.1.call-update) | async-done | bytes 1658896 | tf_op jit(solution)/shard_map/all_gather | solution.py:81
  675.2 6.6 scatter_fusion.1
  681.7 48.0 %all-gather.46.cloned.1.call-done = bf16[1,2304,360]{2,1,0:T(8,128)(2,1)} async-done(((bf16[1,144,360]{2,1,0:T(8,128)(2,1)}), bf16[1,2304,360]{2,1,0:T(8,128)(2,1)}) %all-gather.46.cloned.1.call-update) | async-done | bytes 1658896 | tf_op jit(solution)/shard_map/all_gather | solution.py:69
  731.8 56.8 %all-gather.48.cloned.1.call-done = bf16[1,2304,360]{2,1,0:T(8,128)(2,1)} async-done(((bf16[1,144,360]{2,1,0:T(8,128)(2,1)}), bf16[1,2304,360]{2,1,0:T(8,128)(2,1)}) %all-gather.48.cloned.1.call-update) | async-done | bytes 1658896 | tf_op jit(solution)/shard_map/all_gather | solution.py:70
  788.6 59.5 %all-gather.50.cloned.1.call-done = bf16[1,360,2304]{1,2,0:T(8,128)(2,1)} async-done(((bf16[1,360,144]{1,2,0:T(8,128)(2,1)}), bf16[1,360,2304]{1,2,0:T(8,128)(2,1)}) %all-gather.50.cloned.1.call-update) | async-done | bytes 1658896 | tf_op jit(solution)/shard_map/all_gather | solution.py:81
  852.5 6.5 scatter_fusion.2
  864.3 68.9 %reduce-scatter.4.cloned.1.call-done = bf16[144,256]{1,0:T(8,128)(2,1)} async-done(((bf16[2304,256]{1,0:T(8,128)(2,1)}), bf16[144,256]{1,0:T(8,128)(2,1)}) %reduce-scatter.4.cloned.1.call-update) | async-done | bytes 73744
  935.6 32.5 %psum.22 = f32[4]{0:T(128)S(1)} all-reduce(f32[4]{0:T(128)S(1)} %multiply_reduce_fusion.1), channel_id=1, replica_groups=mesh['dp'=16,'mp'=16] {'mp'}, use_global_device_ids=true, to_apply=%region_35.36 | all-reduce | flops 4 | bytes 32 | tf_op jit(solution)/shard_map/psum | solution.py:98
  968.3 610.6 %all_gather.55 = bf16[256,4,144]{2,1,0:T(4,128)(2,1)S(1)} all-gather(bf16[1,4,144]{2,1,0:T(4,128)(2,1)S(1)} %fusion.79), channel_id=1, replica_groups=mesh['dp'=16,'mp'=16] {'dp','mp'}, dimensions={0}, use_global_device_ids=true | all-gather | bytes 296064 | tf_op jit(solution)/shard_map/all_gather | solution.py:105
  1580.2 101.6 %pmax.7 = f32[64]{0:T(128)S(1)} all-reduce(f32[64]{0:T(128)S(1)} %get-tuple-element.38), channel_id=1, replica_groups=mesh['dp'=16,'mp'=16] {'dp','mp'}, use_global_device_ids=true, to_apply=%region_37.38 | all-reduce | flops 64 | bytes 512 | tf_op jit(solution)/shard_map/pmax | solution.py:114
  1682.0 74.5 %psum.23 = f32[64]{0:T(128)S(1)} all-reduce(f32[64]{0:T(128)S(1)} %exponential_reduce_fusion), channel_id=1, replica_groups=mesh['dp'=16,'mp'=16] {'dp','mp'}, use_global_device_ids=true, to_apply=%region_39.40 | all-reduce | flops 64 | bytes 512 | tf_op jit(solution)/shard_map/psum | solution.py:115
  (172 shorter events, 98.9 us)
Async XLA Ops:
  7.2 1572.4 %copy-start = (bf16[2304,512]{1,0:T(8,128)(2,1)S(1)}, bf16[2304,512]{1,0:T(8,128)(2,1)}, u32[]{:S(2)}) copy-start(bf16[2304,512]{1,0:T(8,128)(2,1)} %param.20) | copy-start | bytes 7077892
  7.2 45.2 %copy-start.5 = (bf16[4,360,144]{1,2,0:T(8,128)(2,1)S(1)}, bf16[4,360,144]{1,2,0:T(8,128)(2,1)}, u32[]{:S(2)}) copy-start(bf16[4,360,144]{1,2,0:T(8,128)(2,1)} %param.18) | copy-start | bytes 1244164
  7.2 120.0 %all-gather.26.cloned.1.call-start = ((), (), s32[]{:S(2)}) async-start(), calls=%async_computation.1 | async-start | bytes 1253376 | tf_op jit(solution)/shard_map/all_gather | solution.py:49
  48.5 150.5 %all-gather.28.cloned.1.call-start = ((), (), s32[]{:S(2)}) async-start(), calls=%async_computation.2 | async-start | bytes 1880064 | tf_op jit(solution)/shard_map/all_gather | solution.py:69
  50.4 76.8 %copy-start.7 = (bf16[2304,4]{0,1:T(4,128)(2,1)S(1)}, bf16[2304,4]{0,1:T(4,128)(2,1)}, u32[]{:S(2)}) copy-start(bf16[2304,4]{0,1:T(4,128)(2,1)} %param.15) | copy-start | bytes 55300
  50.4 207.5 %all-gather.30.cloned.1.call-start = ((), (), s32[]{:S(2)}) async-start(), calls=%async_computation.3 | async-start | bytes 1880064 | tf_op jit(solution)/shard_map/all_gather | solution.py:70
  52.3 264.5 %all-gather.32.cloned.1.call-start = ((), (), s32[]{:S(2)}) async-start(), calls=%async_computation.4 | async-start | bytes 1880064 | tf_op jit(solution)/shard_map/all_gather | solution.py:81
  53.2 322.4 %all-gather.34.cloned.1.call-start = ((), (), s32[]{:S(2)}) async-start(), calls=%async_computation.5 | async-start | bytes 1880064 | tf_op jit(solution)/shard_map/all_gather | solution.py:69
  53.8 380.7 %all-gather.36.cloned.1.call-start = ((), (), s32[]{:S(2)}) async-start(), calls=%async_computation.6 | async-start | bytes 1880064 | tf_op jit(solution)/shard_map/all_gather | solution.py:70
  54.3 439.6 %all-gather.38.cloned.1.call-start = ((), (), s32[]{:S(2)}) async-start(), calls=%async_computation.7 | async-start | bytes 1880064 | tf_op jit(solution)/shard_map/all_gather | solution.py:81
  55.1 497.9 %all-gather.40.cloned.1.call-start = ((), (), s32[]{:S(2)}) async-start(), calls=%async_computation.8 | async-start | bytes 1880064 | tf_op jit(solution)/shard_map/all_gather | solution.py:69
  55.8 556.1 %all-gather.42.cloned.1.call-start = ((), (), s32[]{:S(2)}) async-start(), calls=%async_computation.9 | async-start | bytes 1880064 | tf_op jit(solution)/shard_map/all_gather | solution.py:70
  56.6 614.2 %all-gather.44.cloned.1.call-start = ((), (), s32[]{:S(2)}) async-start(), calls=%async_computation.10 | async-start | bytes 1880064 | tf_op jit(solution)/shard_map/all_gather | solution.py:81
  57.2 672.6 %all-gather.46.cloned.1.call-start = ((), (), s32[]{:S(2)}) async-start(), calls=%async_computation.11 | async-start | bytes 1880064 | tf_op jit(solution)/shard_map/all_gather | solution.py:69
  57.9 730.7 %all-gather.48.cloned.1.call-start = ((), (), s32[]{:S(2)}) async-start(), calls=%async_computation.12 | async-start | bytes 1880064 | tf_op jit(solution)/shard_map/all_gather | solution.py:70
  58.5 789.7 %all-gather.50.cloned.1.call-start = ((), (), s32[]{:S(2)}) async-start(), calls=%async_computation.13 | async-start | bytes 1880064 | tf_op jit(solution)/shard_map/all_gather | solution.py:81
  59.2 873.9 %reduce-scatter.4.cloned.1.call-start = ((), (), s32[]{:S(2)}) async-start(), calls=%async_computation.14 | async-start | bytes 1253376
  83.5 43.6 %copy-start.8 = (s32[160]{0:T(256)}, s32[160]{0:T(256)S(1)}, u32[]{:S(2)}) copy-start(s32[160]{0:T(256)S(1)} %get-tuple-element.31) | copy-start | bytes 1924
  154.2 162.5 %copy-start.4 = (bf16[160,2304]{1,0:T(8,128)(2,1)S(1)}, bf16[160,2304]{1,0:T(8,128)(2,1)}, u32[]{:S(2)}) copy-start(bf16[160,2304]{1,0:T(8,128)(2,1)} %gather_fusion) | copy-start | bytes 2211844
  321.2 54.4 %copy-start.3 = (bf16[160,2304]{1,0:T(8,128)(2,1)S(1)}, bf16[160,2304]{1,0:T(8,128)(2,1)}, u32[]{:S(2)}) copy-start(bf16[160,2304]{1,0:T(8,128)(2,1)} %gather_fusion.2) | copy-start | bytes 2211844
  498.4 54.6 %copy-start.2 = (bf16[160,2304]{1,0:T(8,128)(2,1)S(1)}, bf16[160,2304]{1,0:T(8,128)(2,1)}, u32[]{:S(2)}) copy-start(bf16[160,2304]{1,0:T(8,128)(2,1)} %gather_fusion.4) | copy-start | bytes 2211844
  555.0 120.2 %copy-start.11 = (s32[160]{0:T(256)S(1)}, s32[160]{0:T(256)}, u32[]{:S(2)}) copy-start(s32[160]{0:T(256)} %copy-done.10) | copy-start | bytes 1924
  675.2 54.6 %copy-start.1 = (bf16[160,2304]{1,0:T(8,128)(2,1)S(1)}, bf16[160,2304]{1,0:T(8,128)(2,1)}, u32[]{:S(2)}) copy-start(bf16[160,2304]{1,0:T(8,128)(2,1)} %gather_fusion.6) | copy-start | bytes 2211844
  731.8 120.7 %copy-start.9 = (s32[160]{0:T(256)S(1)}, s32[160]{0:T(256)}, u32[]{:S(2)}) copy-start(s32[160]{0:T(256)} %copy-done.8) | copy-start | bytes 1924
  (7 other events, 25.2 us)
Sparse Core Ops, SparseCore 0:
  48.6 78.5 all-gather.25
  129.8 69.1 all-gather.27
  201.6 56.3 all-gather.29
  260.4 56.3 all-gather.31
  319.2 56.3 all-gather.33
  378.1 56.3 all-gather.35
  437.6 56.3 all-gather.37
  496.6 56.3 all-gather.39
  555.6 56.3 all-gather.41
  614.4 56.3 all-gather.43
  673.4 56.3 all-gather.45
  732.2 56.3 all-gather.47
  791.8 56.3 all-gather.49
  862.3 70.7 reduce-scatter.3
where the time goes:
time: 1770 us; the launch traced here: 1760 us
  blocking collectives  858 us (48%)
  waiting for transfers between devices  769 us (43%)
  local copies, waits for them, and re-layouts  56.7 us (3%)
  other arithmetic  37.7 us (2%)
  matrix products  28 us (2%)
    all_gather x1, blocking collectives, body(): lax.all_gather(end_normed[None], ('dp', 'mp'), axis=0, tiled=True)  611 us
    all_gather x4, waiting for transfers between devices, body(): lax.all_gather(specialist_contract_weights[expert], 'dp', axis=1, tiled=T...  237 us
    all_gather x4, waiting for transfers between devices, body(): lax.all_gather(specialist_expand_weights[expert], 'dp', axis=0, tiled=True)  227 us
    all_gather x4, waiting for transfers between devices, body(): lax.all_gather(specialist_switch_weights[expert], 'dp', axis=0, tiled=True)  187 us
    pmax x1, blocking collectives, body(): largest = lax.pmax(jnp.max(lexicon_logit_values, axis=1), ('dp', 'mp'))  102 us
    unnamed x15, waiting for transfers between devices  74.5 us
    psum x1, blocking collectives, body(): lax.psum(jnp.sum(jnp.exp(lexicon_logit_values - largest[:, None]), axis=1...  74.5 us
    all_gather x1, waiting for transfers between devices, body(): features = lax.all_gather(normed_local, 'mp', axis=1, tiled=True)  43 us
  transfers between devices with their start and end apart: 14, of which 14 were waited for; matrix products, arithmetic and copies ran while one was open for 6% of the time, Pallas kernels for 0%

commit v1 on v0

--- a/solution.py
+++ b/solution.py
@@ -46,7 +46,9 @@
         * lax.rsqrt(squares / EMBED_DIMENSION + epsilon)[:, None]
         * premix_rmsnorm_gain
     ).astype(jnp.bfloat16)
-    features = lax.all_gather(normed_local, "mp", axis=1, tiled=True)
+    features = jnp.concatenate(
+        lax.all_to_all(jnp.stack([normed_local] * lax.axis_size("mp")), "mp", 0, 0), axis=1
+    )
     router = jnp.dot(features, dispatcher_weights, preferred_element_type=jnp.float32)
     mixing = jax.nn.softmax(jnp.take_along_axis(router, chosen_specialists, axis=1), axis=1)
     tables = [slot_tables(chosen_specialists, expert, CAP) for expert in range(experts)]

time: 1770 us -> 1650 us (0.932)
  waiting for transfers between devices: 769 us -> 622 us
    all_gather x4, waiting for transfers between devices: 227 us -> 171 us  [body(): lax.all_gather(specialist_expand_weights[expert], 'dp', axis=0, tiled=True)]
    all_gather x1 -> x0, waiting for transfers between devices: 43 us -> none  [body(): features = lax.all_gather(normed_local, 'mp', axis=1, tiled=True)]
    all_gather x4, waiting for transfers between devices: 187 us -> 145 us  [body(): lax.all_gather(specialist_switch_weights[expert], 'dp', axis=0, tiled=True)]
    unnamed x15 -> x14, waiting for transfers between devices: 74.5 us -> 75.4 us
  transfers between devices with their start and end apart: 14 -> 14, of which waited for: 14 -> 11; matrix products, arithmetic and copies ran while one was open for 6% -> 7% of each run, Pallas kernels for 0% -> 0%
where the time goes in v1:
time: 1650 us; the launch traced here: 1640 us
  blocking collectives  857 us (52%)
  waiting for transfers between devices  622 us (38%)
  local copies, waits for them, and re-layouts  68.7 us (4%)
  other arithmetic  46.8 us (3%)
  matrix products  27.9 us (2%)
    all_gather x1, blocking collectives, body(): lax.all_gather(end_normed[None], ('dp', 'mp'), axis=0, tiled=True)  610 us
    all_gather x4, waiting for transfers between devices, body(): lax.all_gather(specialist_contract_weights[expert], 'dp', axis=1, tiled=T...  231 us
    all_gather x4, waiting for transfers between devices, body(): lax.all_gather(specialist_expand_weights[expert], 'dp', axis=0, tiled=True)  171 us
    all_gather x4, waiting for transfers between devices, body(): lax.all_gather(specialist_switch_weights[expert], 'dp', axis=0, tiled=True)  145 us
    pmax x1, blocking collectives, body(): largest = lax.pmax(jnp.max(lexicon_logit_values, axis=1), ('dp', 'mp'))  102 us
    unnamed x14, waiting for transfers between devices  75.4 us
    psum x1, blocking collectives, body(): lax.psum(jnp.sum(jnp.exp(lexicon_logit_values - largest[:, None]), axis=1...  74.5 us
    psum x1, blocking collectives, body(): lax.psum(jnp.sum(skip_stream_arriving * skip_stream_arriving, axis=1), 'mp')  38.5 us
  transfers between devices with their start and end apart: 14, of which 11 were waited for; matrix products, arithmetic and copies ran while one was open for 7% of the time, Pallas kernels for 0%

profile of v1, /device:TPU:1, one launch (start us, length us, event | category | flops | bytes accessed | tf_op | source)
XLA Modules:
  0.0 1640.6 jit_solution(15547742844517644709)
XLA Ops:
  17.4 38.5 %psum.21 = f32[256]{0:T(256)S(1)} all-reduce(f32[256]{0:T(256)S(1)} %multiply_reduce_fusion), channel_id=1, replica_groups=mesh['dp'=16,'mp'=16] {'mp'}, use_global_device_ids=true, to_apply=%region_5.6 | all-reduce | flops 256 | bytes 2048 | tf_op jit(solution)/shard_map/psum | solution.py:43
  110.2 4.9 gather_fusion.9
  140.7 53.3 %all-gather.29.cloned.1.call-done = bf16[1,360,2304]{1,2,0:T(8,128)(2,1)} async-done(((bf16[1,360,144]{1,2,0:T(8,128)(2,1)}), bf16[1,360,2304]{1,2,0:T(8,128)(2,1)}) %all-gather.29.cloned.1.call-update) | async-done | bytes 1658896 | tf_op jit(solution)/shard_map/all_gather | solution.py:83
  194.1 4.4 convolution_multiply_fusion.3
  198.5 5.2 scatter_custom_fusion.3
  203.7 49.3 %all-gather.31.cloned.1.call-done = bf16[1,2304,360]{2,1,0:T(8,128)(2,1)} async-done(((bf16[1,144,360]{2,1,0:T(8,128)(2,1)}), bf16[1,2304,360]{2,1,0:T(8,128)(2,1)}) %all-gather.31.cloned.1.call-update) | async-done | bytes 1658896 | tf_op jit(solution)/shard_map/all_gather | solution.py:71
  255.0 56.8 %all-gather.33.cloned.1.call-done = bf16[1,2304,360]{2,1,0:T(8,128)(2,1)} async-done(((bf16[1,144,360]{2,1,0:T(8,128)(2,1)}), bf16[1,2304,360]{2,1,0:T(8,128)(2,1)}) %all-gather.33.cloned.1.call-update) | async-done | bytes 1658896 | tf_op jit(solution)/shard_map/all_gather | solution.py:72
  311.8 58.8 %all-gather.35.cloned.1.call-done = bf16[1,360,2304]{1,2,0:T(8,128)(2,1)} async-done(((bf16[1,360,144]{1,2,0:T(8,128)(2,1)}), bf16[1,360,2304]{1,2,0:T(8,128)(2,1)}) %all-gather.35.cloned.1.call-update) | async-done | bytes 1658896 | tf_op jit(solution)/shard_map/all_gather | solution.py:83
  374.9 6.5 scatter_fusion
  381.5 48.1 %all-gather.37.cloned.1.call-done = bf16[1,2304,360]{2,1,0:T(8,128)(2,1)} async-done(((bf16[1,144,360]{2,1,0:T(8,128)(2,1)}), bf16[1,2304,360]{2,1,0:T(8,128)(2,1)}) %all-gather.37.cloned.1.call-update) | async-done | bytes 1658896 | tf_op jit(solution)/shard_map/all_gather | solution.py:71
  431.6 56.9 %all-gather.39.cloned.1.call-done = bf16[1,2304,360]{2,1,0:T(8,128)(2,1)} async-done(((bf16[1,144,360]{2,1,0:T(8,128)(2,1)}), bf16[1,2304,360]{2,1,0:T(8,128)(2,1)}) %all-gather.39.cloned.1.call-update) | async-done | bytes 1658896 | tf_op jit(solution)/shard_map/all_gather | solution.py:72
  488.5 59.0 %all-gather.41.cloned.1.call-done = bf16[1,360,2304]{1,2,0:T(8,128)(2,1)} async-done(((bf16[1,360,144]{1,2,0:T(8,128)(2,1)}), bf16[1,360,2304]{1,2,0:T(8,128)(2,1)}) %all-gather.41.cloned.1.call-update) | async-done | bytes 1658896 | tf_op jit(solution)/shard_map/all_gather | solution.py:83
  547.5 4.4 convolution_multiply_fusion.1
  551.9 6.5 scatter_fusion.1
  558.5 47.9 %all-gather.43.cloned.1.call-done = bf16[1,2304,360]{2,1,0:T(8,128)(2,1)} async-done(((bf16[1,144,360]{2,1,0:T(8,128)(2,1)}), bf16[1,2304,360]{2,1,0:T(8,128)(2,1)}) %all-gather.43.cloned.1.call-update) | async-done | bytes 1658896 | tf_op jit(solution)/shard_map/all_gather | solution.py:71
  608.4 57.0 %all-gather.45.cloned.1.call-done = bf16[1,2304,360]{2,1,0:T(8,128)(2,1)} async-done(((bf16[1,144,360]{2,1,0:T(8,128)(2,1)}), bf16[1,2304,360]{2,1,0:T(8,128)(2,1)}) %all-gather.45.cloned.1.call-update) | async-done | bytes 1658896 | tf_op jit(solution)/shard_map/all_gather | solution.py:72
  665.3 59.4 %all-gather.47.cloned.1.call-done = bf16[1,360,2304]{1,2,0:T(8,128)(2,1)} async-done(((bf16[1,360,144]{1,2,0:T(8,128)(2,1)}), bf16[1,360,2304]{1,2,0:T(8,128)(2,1)}) %all-gather.47.cloned.1.call-update) | async-done | bytes 1658896 | tf_op jit(solution)/shard_map/all_gather | solution.py:83
  724.7 4.4 convolution_multiply_fusion
  729.1 6.5 scatter_fusion.2
  740.9 70.0 %reduce-scatter.4.cloned.1.call-done = bf16[144,256]{1,0:T(8,128)(2,1)} async-done(((bf16[2304,256]{1,0:T(8,128)(2,1)}), bf16[144,256]{1,0:T(8,128)(2,1)}) %reduce-scatter.4.cloned.1.call-update) | async-done | bytes 73744
  813.4 31.6 %psum.22 = f32[4]{0:T(128)S(1)} all-reduce(f32[4]{0:T(128)S(1)} %multiply_reduce_fusion.1), channel_id=1, replica_groups=mesh['dp'=16,'mp'=16] {'mp'}, use_global_device_ids=true, to_apply=%region_35.36 | all-reduce | flops 4 | bytes 32 | tf_op jit(solution)/shard_map/psum | solution.py:100
  845.1 610.4 %all_gather.51 = bf16[256,4,144]{2,1,0:T(4,128)(2,1)S(1)} all-gather(bf16[1,4,144]{2,1,0:T(4,128)(2,1)S(1)} %fusion.79), channel_id=1, replica_groups=mesh['dp'=16,'mp'=16] {'dp','mp'}, dimensions={0}, use_global_device_ids=true | all-gather | bytes 296064 | tf_op jit(solution)/shard_map/all_gather | solution.py:107
  1456.8 101.6 %pmax.7 = f32[64]{0:T(128)S(1)} all-reduce(f32[64]{0:T(128)S(1)} %get-tuple-element.38), channel_id=1, replica_groups=mesh['dp'=16,'mp'=16] {'dp','mp'}, use_global_device_ids=true, to_apply=%region_37.38 | all-reduce | flops 64 | bytes 512 | tf_op jit(solution)/shard_map/pmax | solution.py:116
  1558.6 74.5 %psum.23 = f32[64]{0:T(128)S(1)} all-reduce(f32[64]{0:T(128)S(1)} %exponential_reduce_fusion), channel_id=1, replica_groups=mesh['dp'=16,'mp'=16] {'dp','mp'}, use_global_device_ids=true, to_apply=%region_39.40 | all-reduce | flops 64 | bytes 512 | tf_op jit(solution)/shard_map/psum | solution.py:117
  (190 shorter events, 110.2 us)
Async XLA Ops:
  7.2 1449.0 %copy-start = (bf16[2304,512]{1,0:T(8,128)(2,1)S(1)}, bf16[2304,512]{1,0:T(8,128)(2,1)}, u32[]{:S(2)}) copy-start(bf16[2304,512]{1,0:T(8,128)(2,1)} %param.20) | copy-start | bytes 7077892
  7.2 10.2 copy-start.8
  7.2 131.3 %all-gather.25.cloned.1.call-start = ((), (), s32[]{:S(2)}) async-start(), calls=%async_computation.2 | async-start | bytes 1880064 | tf_op jit(solution)/shard_map/all_gather | solution.py:71
  9.3 46.7 %copy-start.21 = (f32[144]{0:T(256)S(1)}, f32[144]{0:T(256)}, u32[]{:S(2)}) copy-start(f32[144]{0:T(256)} %param.14) | copy-start | bytes 1732
  9.3 131.5 %all-gather.27.cloned.1.call-start = ((), (), s32[]{:S(2)}) async-start(), calls=%async_computation.3 | async-start | bytes 1880064 | tf_op jit(solution)/shard_map/all_gather | solution.py:72
  11.2 182.9 %all-gather.29.cloned.1.call-start = ((), (), s32[]{:S(2)}) async-start(), calls=%async_computation.4 | async-start | bytes 1880064 | tf_op jit(solution)/shard_map/all_gather | solution.py:83
  12.1 240.8 %all-gather.31.cloned.1.call-start = ((), (), s32[]{:S(2)}) async-start(), calls=%async_computation.5 | async-start | bytes 1880064 | tf_op jit(solution)/shard_map/all_gather | solution.py:71
  12.7 299.1 %all-gather.33.cloned.1.call-start = ((), (), s32[]{:S(2)}) async-start(), calls=%async_computation.6 | async-start | bytes 1880064 | tf_op jit(solution)/shard_map/all_gather | solution.py:72
  13.3 357.3 %all-gather.35.cloned.1.call-start = ((), (), s32[]{:S(2)}) async-start(), calls=%async_computation.7 | async-start | bytes 1880064 | tf_op jit(solution)/shard_map/all_gather | solution.py:83
  13.8 415.7 %all-gather.37.cloned.1.call-start = ((), (), s32[]{:S(2)}) async-start(), calls=%async_computation.8 | async-start | bytes 1880064 | tf_op jit(solution)/shard_map/all_gather | solution.py:71
  14.6 473.9 %all-gather.39.cloned.1.call-start = ((), (), s32[]{:S(2)}) async-start(), calls=%async_computation.9 | async-start | bytes 1880064 | tf_op jit(solution)/shard_map/all_gather | solution.py:72
  15.3 532.2 %all-gather.41.cloned.1.call-start = ((), (), s32[]{:S(2)}) async-start(), calls=%async_computation.10 | async-start | bytes 1880064 | tf_op jit(solution)/shard_map/all_gather | solution.py:83
  16.1 590.3 %all-gather.43.cloned.1.call-start = ((), (), s32[]{:S(2)}) async-start(), calls=%async_computation.11 | async-start | bytes 1880064 | tf_op jit(solution)/shard_map/all_gather | solution.py:71
  16.7 648.7 %all-gather.45.cloned.1.call-start = ((), (), s32[]{:S(2)}) async-start(), calls=%async_computation.12 | async-start | bytes 1880064 | tf_op jit(solution)/shard_map/all_gather | solution.py:72
  57.2 48.9 %all-to-all-start = ((bf16[16,256,144]{1,2,0:T(8,128)(2,1)}), bf16[16,256,144]{1,2,0:T(8,128)(2,1)S(1)}, u32[]{:S(2)}, u32[]{:S(2)}) async-start(bf16[16,256,144]{1,2,0:T(8,128)(2,1)} %stack.2), calls=%async_computation | async-start | bytes 2359296 | tf_op jit(solution)/shard_map/all_to_all | solution.py:50
  60.9 663.9 %all-gather.47.cloned.1.call-start = ((), (), s32[]{:S(2)}) async-start(), calls=%async_computation.13 | async-start | bytes 1880064 | tf_op jit(solution)/shard_map/all_gather | solution.py:83
  61.5 749.4 %reduce-scatter.4.cloned.1.call-start = ((), (), s32[]{:S(2)}) async-start(), calls=%async_computation.14 | async-start | bytes 1253376
  135.8 58.3 %copy-start.7 = (bf16[160,2304]{1,0:T(8,128)(2,1)S(1)}, bf16[160,2304]{1,0:T(8,128)(2,1)}, u32[]{:S(2)}) copy-start(bf16[160,2304]{1,0:T(8,128)(2,1)} %gather_fusion) | copy-start | bytes 2211844
  198.5 54.4 %copy-start.6 = (bf16[160,2304]{1,0:T(8,128)(2,1)S(1)}, bf16[160,2304]{1,0:T(8,128)(2,1)}, u32[]{:S(2)}) copy-start(bf16[160,2304]{1,0:T(8,128)(2,1)} %gather_fusion.2) | copy-start | bytes 2211844
  255.0 120.0 %copy-start.16 = (s32[160]{0:T(256)S(1)}, s32[160]{0:T(256)}, u32[]{:S(2)}) copy-start(s32[160]{0:T(256)} %copy-done.15) | copy-start | bytes 1924
  374.9 54.6 %copy-start.5 = (bf16[160,2304]{1,0:T(8,128)(2,1)S(1)}, bf16[160,2304]{1,0:T(8,128)(2,1)}, u32[]{:S(2)}) copy-start(bf16[160,2304]{1,0:T(8,128)(2,1)} %gather_fusion.4) | copy-start | bytes 2211844
  431.6 120.3 %copy-start.14 = (s32[160]{0:T(256)S(1)}, s32[160]{0:T(256)}, u32[]{:S(2)}) copy-start(s32[160]{0:T(256)} %copy-done.13) | copy-start | bytes 1924
  551.9 54.5 %copy-start.4 = (bf16[160,2304]{1,0:T(8,128)(2,1)S(1)}, bf16[160,2304]{1,0:T(8,128)(2,1)}, u32[]{:S(2)}) copy-start(bf16[160,2304]{1,0:T(8,128)(2,1)} %gather_fusion.6) | copy-start | bytes 2211844
  608.4 120.8 %copy-start.12 = (s32[160]{0:T(256)S(1)}, s32[160]{0:T(256)}, u32[]{:S(2)}) copy-start(s32[160]{0:T(256)} %copy-done.11) | copy-start | bytes 1924
  (16 other events, 47.3 us)
Sparse Core Ops, SparseCore 0:
  10.7 65.2 all-gather.24
  78.5 56.5 all-gather.26
  137.7 56.3 all-gather.28
  196.6 56.3 all-gather.30
  255.4 56.3 all-gather.32
  314.2 56.3 all-gather.34
  373.2 56.3 all-gather.36
  432.2 56.3 all-gather.38
  491.2 56.3 all-gather.40
  550.0 56.3 all-gather.42
  609.0 56.3 all-gather.44
  668.4 56.3 all-gather.46
  739.0 71.8 reduce-scatter.3
